TPU v7x, 512 devices: a whole 4x4x16 slice. The times are simulated.
512 devices in a mesh: ctx: 32 (over z, y_lo), exp: 16 (over y_hi, x, core).
Axes of the slice: x: 4, y: 4 (y_hi: 2, y_lo: 2; y = y_hi * 2 + y_lo), z: 16, core: 2. Of those that a mesh axis runs over, the one named last changes fastest.
Arguments:
- queries: bfloat16 [4096, 64, 576], P('ctx', 'exp'), may hold values from -300 to 300
- latents: bfloat16 [4096, 576], P('ctx'), may hold values from -6 to 6
- value_up: bfloat16 [64, 512, 128], P('exp'), may hold values from -0.5 to 0.5
- out_weight: bfloat16 [8192, 7168], P('exp', 'ctx'), may hold values from -0.125 to 0.125
Outputs:
- attn_out: bfloat16 [4096, 7168], P(('ctx', 'exp'))
All inputs are finite; a program needn't handle non-finite values.
Results may differ from a plain program's by a relative error of at most 0.014.
Values may be sent and summed in bfloat16 or wider, within the bound.
A program may use at most 64 MiB of HBM per device.

v0:
```python
import jax
import jax.numpy as jnp
from jax import lax
from jax.sharding import PartitionSpec as P

VLAT = 512


score_scale = 192.0 ** (-0.5)


def update(carry, piece, query_rows, row_pos):
    run_max, run_total, accum = carry
    key_pos = jnp.arange(piece.shape[0])
    scores = (
        lax.dot_general(
            query_rows, piece, (((1,), (1,)), ((), ())), preferred_element_type=jnp.float32
        )
        * score_scale
    )
    visible = key_pos[None, :] <= row_pos[:, None]
    scores = jnp.where(visible, scores, -1e30)
    new_max = jnp.maximum(run_max, jnp.max(scores, axis=1))
    expo = jnp.where(visible, jnp.exp(scores - new_max[:, None]), 0.0)
    run_total = jnp.sum(expo, axis=1)
    accum = jnp.dot(expo.astype(jnp.bfloat16), piece[:, :VLAT], preferred_element_type=jnp.float32)
    return (new_max, run_total, accum)


def initial_state(nrows):
    return (
        jnp.full((nrows,), -1e30, jnp.float32),
        jnp.zeros((nrows,), jnp.float32),
        jnp.zeros((nrows, VLAT), jnp.float32),
    )


def shards(queries, latents, value_up, out_weight):
    tok_rows = queries.shape[0]
    head_count = queries.shape[1]
    lat_width = queries.shape[2]
    nrows = tok_rows * head_count
    first_row = lax.axis_index("ctx") * tok_rows
    query_rows = queries.reshape(nrows, lat_width)
    row_pos = first_row + jnp.arange(nrows) // head_count
    start_state = initial_state(nrows)
    folded = update(
        start_state, lax.all_gather(latents, "ctx", axis=0, tiled=True), query_rows, row_pos
    )
    run_max, run_total, accum = folded
    context = (accum / run_total[:, None]).astype(jnp.bfloat16).reshape(tok_rows, head_count, VLAT)
    values = jnp.einsum(
        "thc,hcd->thd", context, value_up, preferred_element_type=jnp.float32
    ).astype(jnp.bfloat16)
    values = values.reshape(tok_rows, head_count * value_up.shape[2])
    partial_out = jnp.dot(
        values,
        lax.all_gather(out_weight, "ctx", axis=1, tiled=True),
        preferred_element_type=jnp.float32,
    )
    return lax.psum_scatter(
        partial_out.astype(jnp.bfloat16), "exp", scatter_dimension=0, tiled=True
    )


def solution(mesh):
    in_specs = (P("ctx", "exp", None), P("ctx", None), P("exp", None, None), P("exp", "ctx"))
    out_specs = P(("ctx", "exp"), None)
    return jax.shard_map(shards, mesh=mesh, in_specs=in_specs, out_specs=out_specs, check_vma=False)
```

profile of v0, /device:TPU:1, one launch (start us, length us, event | category | flops | bytes accessed | tf_op | source)
XLA Modules:
  0.0 462.5 jit_solution(15281399740298661983)
XLA Ops:
  6.5 0.0 copy-start
  6.5 0.0 all-gather.3.cloned.1.call-start
  6.5 0.7 all-gather.3.cloned.1.call-update
  7.3 0.0 all-gather.5.cloned.1.call-start
  7.3 0.7 all-gather.5.cloned.1.call-update
  8.0 0.0 reduce-scatter.2.cloned.1.call-start
  8.1 1.6 copy.7
  9.7 0.3 reshape.27
  10.0 151.6 %all-gather.3.cloned.1.call-done = bf16[4096,576]{0,1:T(8,128)(2,1)} async-done(((bf16[128,576]{0,1:T(8,128)(2,1)}), bf16[4096,576]{0,1:T(8,128)(2,1)}) %all-gather.3.cloned.1.call-update) | async-done | bytes 4718608 | tf_op jit(solution)/shard_map/all_gather | solution.py:48
  161.6 6.1 %fusion = (f32[512]{0:T(512)S(1)}, f32[512,4096]{1,0:T(8,128)S(1)}) fusion(s32[512]{0:T(512)S(1)} %fusion.15, bf16[512,576]{1,0:T(8,128)(2,1)S(1)} %reshape.27, bf16[4096,576]{0,1:T(8,128)(2,1)} %all-gather.3.cloned.1.call-done), kind=kOutput, calls=%fused_computation.4 | convolution fusion | flops 2424307200 | bytes 13701120 | tf_op jit(solution)/shard_map/dot_general | solution.py:16
  167.7 0.0 copy-start.1
  167.8 2.8 fusion.1
  170.6 0.0 copy-done.1
  170.6 3.0 divide_convert_fusion
  173.6 0.1 reshape.28
  173.8 0.0 copy-done
  173.8 0.3 convolution_convert_fusion.1
  174.1 182.2 %all-gather.5.cloned.1.call-done = bf16[512,7168]{0,1:T(8,128)(2,1)} async-done(((bf16[512,224]{0,1:T(8,128)(2,1)}), bf16[512,7168]{0,1:T(8,128)(2,1)}) %all-gather.5.cloned.1.call-update) | async-done | bytes 7340048 | tf_op jit(solution)/shard_map/all_gather | solution.py:58
  356.4 6.9 %convolution_convert_fusion = bf16[128,7168]{1,0:T(8,128)(2,1)} fusion(bf16[128,512]{0,1:T(8,128)(2,1)S(1)} %bitcast.8, bf16[512,7168]{0,1:T(8,128)(2,1)} %all-gather.5.cloned.1.call-done), kind=kOutput, calls=%fused_computation | convolution fusion | flops 940441600 | bytes 9306112 | tf_op jit(solution)/shard_map/dot_general | solution.py:56
  363.2 0.0 reduce-scatter.2.cloned.1.call-update
  363.3 92.7 %reduce-scatter.2.cloned.1.call-done = bf16[8,7168]{1,0:T(8,128)(2,1)} async-done(((bf16[128,7168]{1,0:T(8,128)(2,1)}), bf16[8,7168]{1,0:T(8,128)(2,1)}) %reduce-scatter.2.cloned.1.call-update) | async-done | bytes 114704 | tf_op jit(solution)/shard_map/reduce_scatter | solution.py:61
  (2 shorter events, 0.0 us)
Async XLA Ops:
  6.5 167.2 %copy-start = (bf16[4,512,128]{2,1,0:T(8,128)(2,1)S(1)}, bf16[4,512,128]{2,1,0:T(8,128)(2,1)}, u32[]{:S(2)}) copy-start(bf16[4,512,128]{2,1,0:T(8,128)(2,1)} %param.6) | copy-start | bytes 1572868
  6.5 155.1 %all-gather.3.cloned.1.call-start = ((), (), s32[]{:S(2)}) async-start(), calls=%async_computation.1 | async-start | bytes 4866048 | tf_op jit(solution)/shard_map/all_gather | solution.py:48
  7.3 349.1 %all-gather.5.cloned.1.call-start = ((), (), s32[]{:S(2)}) async-start(), calls=%async_computation.2 | async-start | bytes 7569408 | tf_op jit(solution)/shard_map/all_gather | solution.py:58
  8.0 447.9 %reduce-scatter.2.cloned.1.call-start = ((), (), s32[]{:S(2)}) async-start(), calls=%async_computation.3 | async-start | bytes 1949696 | tf_op jit(solution)/shard_map/reduce_scatter | solution.py:61
  167.7 2.9 copy-start.1
Sparse Core Ops, SparseCore 0:
  9.3 152.2 all-gather.2
  163.7 192.5 all-gather.4
  363.4 92.4 reduce-scatter.1
where the time goes:
time: 463 us; the launch traced here: 462 us
  waiting for transfers between devices  428 us (92%)
  matrix products  16.3 us (4%)
  between operations  13.2 us (3%)
    all_gather x1, waiting for transfers between devices, shards(): lax.all_gather(out_weight, 'ctx', axis=1, tiled=True)  182 us
    all_gather x1, waiting for transfers between devices, shards(): lax.all_gather(latents, 'ctx', axis=0, tiled=True)  152 us
    reduce_scatter x1, waiting for transfers between devices, shards(): lax.psum_scatter(partial_out.astype(jnp.bfloat16), 'exp', scatter_dimensi...  92.7 us
  transfers between devices with their start and end apart: 3, of which 3 were waited for; matrix products, arithmetic and copies ran while one was open for 3% of the time, Pallas kernels for 0%

commit v1 on v0

v1 whole, which is shorter than its diff:
```python
import functools

import jax
import jax.numpy as jnp
from jax import lax
from jax.experimental import pallas as pl
from jax.experimental.pallas import tpu as pltpu
from jax.sharding import PartitionSpec as P

MESH = pl.DeviceIdType.MESH
LANES = 128
GROUP = 4
LOG2E = 1.4426950408889634
score_scale = 192.0 ** (-0.5)
LOW = -1e30


def kernel(
    nz, nx, nvl, nb,
    q_ref, lat_ref, up_ref, w_ref, out_ref,
    lat_s, wab, m_s, l_s, acc, vx, ps, cr, xs, xr, ys, yr,
    zl_s, zl_r, yf_s, yf_r, ce_s, ce_r, co_s, co_r,
    za_s, za_r, zb_s, zb_r, v_s, v_r, c_s, c_r, x_s, x_r, y_s, y_r,
):
    half = nz // 2
    tok = lat_ref.shape[0]
    hrow = tok // 2
    heads = up_ref.shape[0]
    vd = up_ref.shape[2]
    sub = nb // 2
    n_a = nz // GROUP
    n_groups = 2 * n_a

    ctx, ex = lax.axis_index("ctx"), lax.axis_index("exp")
    z, yl = ctx // 2, ctx % 2
    yh, x, k = ex // (2 * nx), (ex // 2) % nx, ex % 2
    y = yh * 2 + yl

    def dev(zz=z, yy=y, xx=x, kk=k):
        return {"ctx": zz * 2 + yy % 2, "exp": (yy // 2) * (2 * nx) + xx * 2 + kk}

    zn = (dev(zz=(z + 1) % nz), dev(zz=(z + nz - 1) % nz))
    yn = (dev(yy=(y + 1) % 4), dev(yy=(y + 3) % 4))
    core = dev(kk=1 - k)
    ypair = dev(yy=yh * 2 + 1 - yl)
    xn = tuple(((x + dx) % nx, dev(xx=(x + dx) % nx)) for dx in range(1, nx))
    y4 = tuple(((y + dy) % 4, dev(yy=(y + dy) % 4)) for dy in range(1, 4))

    def rc(src, dst, ss, rs, to):
        return pltpu.make_async_remote_copy(
            src_ref=src, dst_ref=dst, send_sem=ss, recv_sem=rs, device_id=to, device_id_type=MESH
        )

    def zc(d, s):
        return (z + nz - s) % nz if d == 0 else (z + s) % nz

    def slot(c, yy, kk):
        return lat_s.at[c, pl.ds(pl.multiple_of(yy * tok + kk * hrow, hrow), hrow)]

    own_half = lat_ref.at[pl.ds(pl.multiple_of(k * hrow, hrow), hrow)]

    def zl(d, s, src=None):
        at = slot(zc(d, s), yl, k)
        return rc(at if src is None else src, at, zl_s.at[d, s], zl_r.at[d, s], zn[d])

    def zl_in(d, s):
        at = slot(zc(d, s), yl, k)
        return rc(at, at, zl_s.at[d, s - 1], zl_r.at[d, s - 1], zn[d])

    def yf(d, s, src=None):
        at = slot(zc(d, s), yl, k)
        return rc(at if src is None else src, at, yf_s.at[d, s], yf_r.at[d, s], yn[d])

    def yf_in(d, s):
        at = slot(zc(d, s), 1 - yl, k)
        return rc(at, at, yf_s.at[d, s], yf_r.at[d, s], yn[d])

    def ce(d, s):
        at = slot(zc(d, s), yl, k)
        return rc(at, at, ce_s.at[d, s], ce_r.at[d, s], core)

    def ce_in(d, s):
        at = slot(zc(d, s), yl, 1 - k)
        return rc(at, at, ce_s.at[d, s], ce_r.at[d, s], core)

    def co(d, s):
        at = slot(zc(d, s), 1 - yl, k)
        return rc(at, at, co_s.at[d, s], co_r.at[d, s], core)

    def co_in(d, s):
        at = slot(zc(d, s), 1 - yl, 1 - k)
        return rc(at, at, co_s.at[d, s], co_r.at[d, s], core)

    def za(d, s, src=None, back=0):
        at = wab.at[0, zc(d, s)]
        return rc(at if src is None else src, at, za_s.at[d, s - back], za_r.at[d, s - back], zn[d])

    def zb(d, p, s, src=None, back=0):
        at = wab.at[1, zc(d, s), pl.ds(p * sub, sub)]
        return rc(
            at if src is None else src, at, zb_s.at[d, p, s - back], zb_r.at[d, p, s - back], zn[d]
        )

    barrier = pltpu.get_barrier_semaphore()
    peers = [zn[0], zn[1], core] + [t for _, t in xn] + [t for _, t in y4]
    for peer in peers:
        pl.semaphore_signal(barrier, inc=1, device_id=peer, device_id_type=MESH)
    pl.semaphore_wait(barrier, len(peers))

    for d in range(2):
        zl(d, 0, own_half).start()
    yf(0, 0, own_half).start()
    for d in range(2):
        za(d, 0, w_ref.at[0]).start()

    lat_s[z, pl.ds(pl.multiple_of(yl * tok, tok), tok)] = lat_ref[...]
    wab[0, z] = w_ref[0]
    wab[1, z] = w_ref[1]
    if nb < LANES:
        wab[1, :, nb:] = jnp.zeros((nz, LANES - nb, wab.shape[3]), wab.dtype)
    m_s[...] = jnp.full_like(m_s, LOW)
    l_s[...] = jnp.zeros_like(l_s)
    acc[...] = jnp.zeros_like(acc)

    def attend(c):
        keys = lat_s[c]
        scores = lax.dot_general(
            q_ref[...], keys, (((1,), (1,)), ((), ())), preferred_element_type=jnp.float32
        ) * (score_scale * LOG2E)
        rows, cols = scores.shape
        row_pos = z * cols + yl * tok + lax.broadcasted_iota(jnp.int32, (rows, cols), 0) % tok
        key_pos = c * cols + lax.broadcasted_iota(jnp.int32, (rows, cols), 1)
        scores = jnp.where(key_pos <= row_pos, scores, LOW)
        old = m_s[...]
        new = jnp.maximum(old, jnp.max(scores, axis=1, keepdims=True))
        shrink = jnp.exp2(old - new)
        expo = jnp.exp2(scores - new)
        m_s[...] = new
        l_s[...] = l_s[...] * shrink + jnp.sum(expo, axis=1, keepdims=True)
        acc[...] = acc[...] * shrink + jnp.dot(
            expo.astype(jnp.bfloat16), keys[:, :nvl], preferred_element_type=jnp.float32
        )

    def relay_b(b):
        for d in range(2):
            for p in range(2):
                @pl.when((b >= 1) & ((b < half) | ((b == half) & (k == d))))
                def _():
                    zb(d, p, b, back=1).wait_recv()

                @pl.when((b >= 1) & ((b < half - 1) | ((b == half - 1) & (k == d))))
                def _():
                    zb(d, p, b).start()

    @pl.loop(1, half + 3)
    def _(s):
        for d in range(2):
            @pl.when((s < half) | ((s == half) & (k == d)))
            def _():
                zl_in(d, s).wait_recv()

                @pl.when((s < half - 1) | ((s == half - 1) & (k == d)))
                def _():
                    zl(d, s).start()

                yf(d, s).start()
                ce(d, s).start()

        s1 = s - 1
        for d in range(2):
            @pl.when(
                ((s1 == 0) & (d == 0)) | ((s1 >= 1) & (s1 < half)) | ((s1 == half) & (k == d))
            )
            def _():
                yf_in(d, s1).wait_recv()
                co(d, s1).start()

        s2 = s - 2
        for d in range(2):
            there = ((s2 >= 1) & (s2 < half)) | ((s2 == half) & (k == 1 - d))

            @pl.when(there)
            def _():
                ce_in(d, s2).wait_recv()

            @pl.when(there | ((s2 == 0) & (d == 0)))
            def _():
                co_in(d, s2).wait_recv()

        @pl.loop(0, 2)
        def _(d):
            c = jnp.where(d == 0, z - s2, z + s2 - nz)

            @pl.when((s2 >= 0) & (c >= 0) & ((d == 0) | ((s2 >= 1) & (s2 < half))))
            def _():
                attend(c)

        for d in range(2):
            @pl.when((s < half) | ((s == half) & (k == d)))
            def _():
                za(d, s, back=1).wait_recv()

                @pl.when((s < half - 1) | ((s == half - 1) & (k == d)))
                def _():
                    za(d, s).start()

        b = s - (half - 1)

        @pl.when(b == 0)
        def _():
            for d in range(2):
                for p in range(2):
                    zb(d, p, 0, w_ref.at[1, pl.ds(p * sub, sub)]).start()

        relay_b(b)

    for h in range(heads):
        rows = pl.ds(h * tok, tok)
        context = (acc[rows, :] / l_s[rows, :]).astype(jnp.bfloat16)
        vx[yl, :, h * vd:(h + 1) * vd] = jnp.dot(
            context, up_ref[h], preferred_element_type=jnp.float32
        ).astype(jnp.bfloat16)

    rc(vx.at[yl], vx.at[yl], v_s, v_r, ypair).start()
    relay_b(jnp.int32(4))
    rc(vx.at[1 - yl], vx.at[1 - yl], v_s, v_r, ypair).wait_recv()

    def block_of(g, j):
        ab = g // n_a
        i = (g % n_a) * GROUP + j
        off = jnp.where(i % 2 == 1, nz - (i + 1) // 2, i // 2)
        return ab, jnp.where(ab == 0, i, (z + off) % nz)

    def c_copy(g):
        return rc(ps.at[g, 1 - k], cr.at[g], c_s.at[g], c_r.at[g], core)

    def x_copy(g, dx):
        at, to = xn[dx]
        return rc(xs.at[g, at], xr.at[g, dx], x_s.at[g, dx], x_r.at[g, dx], to)

    def y_copy(g, dy):
        at, to = y4[dy]
        return rc(ys.at[g, at], yr.at[g, dy], y_s.at[g, dy], y_r.at[g, dy], to)

    def part(g):
        for j in range(GROUP):
            ab, c = block_of(g, j)
            both = vx[...].reshape(2 * tok, vx.shape[2])
            o = lax.dot_general(
                both, wab[ab, c], (((1,), (1,)), ((), ())), preferred_element_type=jnp.float32
            )
            o = o.reshape(2, tok // 16, 2, 8, LANES)
            for kk in range(2):
                piece = jnp.concatenate([o[0, :, kk], o[1, :, kk]], axis=1)
                ps[g, kk, :, j] = piece.astype(jnp.bfloat16)
        c_copy(g).start()

    def sum_cores(g):
        c_copy(g).wait_recv()
        s = ps[g, k].astype(jnp.float32) + cr[g].astype(jnp.float32)
        s = s.astype(jnp.bfloat16)
        for hi in range(2):
            xs[g, :, hi] = s[hi * nx:(hi + 1) * nx]
        for dx in range(nx - 1):
            x_copy(g, dx).start()

    def sum_x(g):
        t = xs[g, x].astype(jnp.float32)
        for dx in range(nx - 1):
            x_copy(g, dx).wait_recv()
            t = t + xr[g, dx].astype(jnp.float32)
        for hi in range(2):
            for lo in range(2):
                ys[g, hi * 2 + lo] = t[hi, :, lo * 8:(lo + 1) * 8]
        for dy in range(3):
            y_copy(g, dy).start()

    def sum_y(g):
        for dy in range(3):
            y_copy(g, dy).wait_recv()
        own = ys[g, y] + yr[g, 1]
        other = yr[g, 0] + yr[g, 2]
        for j in range(GROUP):
            ab, c = block_of(g, j)
            out_ref[ab, 2 * c + yl] = own[j]
            out_ref[ab, 2 * c + 1 - yl] = other[j]

    @pl.loop(0, n_groups + 3)
    def _(i):
        @pl.when(i % 2 == 1)
        def _():
            relay_b(5 + (i - 1) // 2)

        @pl.when(i < n_groups)
        def _():
            part(i)

        @pl.when((i >= 1) & (i < n_groups + 1))
        def _():
            sum_cores(i - 1)

        @pl.when((i >= 2) & (i < n_groups + 2))
        def _():
            sum_x(i - 2)

        @pl.when(i >= 3)
        def _():
            sum_y(i - 3)

    @pl.loop(0, half + 1)
    def _(s):
        for d in range(2):
            @pl.when((s < half - 1) | ((s == half - 1) & (k == d)))
            def _():
                zl(d, s).wait_send()
                za(d, s).wait_send()
                for p in range(2):
                    zb(d, p, s).wait_send()

            got = ((s >= 1) & (s < half)) | ((s == half) & (k == d))

            @pl.when(got)
            def _():
                ce(d, s).wait_send()

            @pl.when(got | ((s == 0) & (d == 0)))
            def _():
                yf(d, s).wait_send()
                co(d, s).wait_send()

    rc(vx.at[yl], vx.at[yl], v_s, v_r, ypair).wait_send()

    @pl.loop(0, n_groups)
    def _(g):
        c_copy(g).wait_send()
        for dx in range(nx - 1):
            x_copy(g, dx).wait_send()
        for dy in range(3):
            y_copy(g, dy).wait_send()


def shards(queries, latents, value_up, out_weight):
    nz = lax.axis_size("ctx") // 2
    nx = lax.axis_size("exp") // 4
    tok, heads, lat = queries.shape
    nvl, vd = value_up.shape[1], value_up.shape[2]
    rows = tok * heads
    width = heads * vd
    ncol = out_weight.shape[1]
    nb = ncol - LANES
    half = nz // 2
    ng = 2 * (nz // GROUP)
    q = jnp.moveaxis(queries, 1, 0).reshape(rows, lat)
    w = jnp.pad(out_weight.T, ((0, 2 * LANES - ncol), (0, 0))).reshape(2, LANES, width)
    bf, f32 = jnp.bfloat16, jnp.float32
    dma = pltpu.SemaphoreType.DMA
    vmem = pl.BlockSpec(memory_space=pltpu.VMEM)
    out = pl.pallas_call(
        functools.partial(kernel, nz, nx, nvl, nb),
        out_shape=jax.ShapeDtypeStruct((2, 2 * nz, 8, LANES), f32),
        in_specs=[vmem] * 4,
        out_specs=vmem,
        scratch_shapes=[
            pltpu.VMEM((nz, 2 * tok, lat), bf),
            pltpu.VMEM((2, nz, LANES, width), bf),
            pltpu.VMEM((rows, 1), f32),
            pltpu.VMEM((rows, 1), f32),
            pltpu.VMEM((rows, nvl), f32),
            pltpu.VMEM((2, tok, width), bf),
            pltpu.VMEM((ng, 2, 2 * nx, GROUP, 16, LANES), bf),
            pltpu.VMEM((ng, 2 * nx, GROUP, 16, LANES), bf),
            pltpu.VMEM((ng, nx, 2, GROUP, 16, LANES), bf),
            pltpu.VMEM((ng, nx - 1, 2, GROUP, 16, LANES), bf),
            pltpu.VMEM((ng, 4, GROUP, 8, LANES), f32),
            pltpu.VMEM((ng, 3, GROUP, 8, LANES), f32),
        ]
        + [dma((2, half + 1))] * 8
        + [dma((2, half))] * 2
        + [dma((2, 2, half))] * 2
        + [dma(())] * 2
        + [dma((ng,))] * 2
        + [dma((ng, nx - 1))] * 2
        + [dma((ng, 3))] * 2,
        compiler_params=pltpu.CompilerParams(
            collective_id=0, has_side_effects=True, vmem_limit_bytes=56 * 2**20
        ),
        name="latent_attention",
    )(q, latents, value_up, w)
    cols = jnp.concatenate([out[0], out[1, :, :, :nb]], axis=2)
    return jnp.moveaxis(cols, 1, 0).reshape(8, 2 * nz * ncol).astype(bf)


def solution(mesh):
    in_specs = (P("ctx", "exp", None), P("ctx", None), P("exp", None, None), P("exp", "ctx"))
    out_specs = P(("ctx", "exp"), None)
    return jax.shard_map(shards, mesh=mesh, in_specs=in_specs, out_specs=out_specs, check_vma=False)
```

time: 463 us -> 108 us (0.23)
  waiting for transfers between devices: 428 us -> 0 us
  Pallas kernels: 0 us -> 102 us
  matrix products: 16.3 us -> 0 us
  between operations: 13.2 us -> 0.05 us
    all_gather x2 -> x0, waiting for transfers between devices: 334 us -> none  [the longest x1 182 us: shards(): lax.all_gather(out_weight, 'ctx', axis=1, tiled=True)]
    pallas_call x0 -> x1, Pallas kernels: none -> 102 us  [shards(): pl.pallas_call(functools.partial(kernel, nz, nx, nvl, nb), out_shape=jax....]
    reduce_scatter x1 -> x0, waiting for transfers between devices: 92.7 us -> none  [shards(): lax.psum_scatter(partial_out.astype(jnp.bfloat16), 'exp', scatter_dimensi...]
    dot_general x4 -> x0, matrix products: 16.3 us -> none  [the longest x1 6.89 us: shards(): jnp.dot(values, lax.all_gather(out_weight, 'ctx', axis=1, tiled=True), pr...]
  transfers between devices with their start and end apart: 3 -> 0, of which waited for: 3 -> 0; matrix products, arithmetic and copies ran while one was open for 3% -> 0% of each run, Pallas kernels for 0% -> 0%
where the time goes in v1:
time: 108 us
  Pallas kernels  102 us (94%)
  local copies, waits for them, and re-layouts  5.41 us (5%)
    pallas_call x1, Pallas kernels, shards(): pl.pallas_call(functools.partial(kernel, nz, nx, nvl, nb), out_shape=jax....  102 us

profile of v1, /device:TPU:1, one launch (start us, length us, event | category | flops | bytes accessed | tf_op | source)
XLA Modules:
  0.0 108.2 jit_solution(14649470170242301992)
XLA Ops:
  0.0 0.0 copy-start
  0.0 1.8 %copy.8.lat_ref = bf16[128,576]{1,0:T(8,128)(2,1)} copy(bf16[128,576]{0,1:T(8,128)(2,1)} %param.5) | data formatting | bytes 294912 | tf_op args[1]
  1.8 1.7 %pad.4 = bf16[256,512]{1,0:T(8,128)(2,1)} pad(bf16[224,512]{1,0:T(8,128)(2,1)} %bitcast.13, bf16[]{:T(256)} %constant.2.clone.1), padding=0_32x0_0 | pad | bytes 491522 | tf_op jit(solution)/shard_map/jit(_pad)/pad | solution.py:354
  3.4 0.0 copy-done
  3.4 1.1 %copy.7 = bf16[4,128,576]{2,1,0:T(8,128)(2,1)} copy(bf16[4,128,576]{1,2,0:T(8,128)(2,1)S(1)} %bitcast.12) | data formatting | bytes 1179648 | tf_op jit(solution)/shard_map/transpose | solution.py:353
  4.5 101.7 %latent_attention.1 = f32[2,32,8,128]{3,2,1,0:T(8,128)} custom-call(bf16[512,576]{1,0:T(8,128)(2,1)} %bitcast.10, bf16[128,576]{1,0:T(8,128)(2,1)} %copy.8.lat_ref, bf16[4,512,128]{2,1,0:T(8,128)(2,1)} %up_ref.1, bf16[2,128,512]{2,1,0:T(8,128)(2,1)} %bitcast.11), custom_call_target="tpu_custom_call" | custom-call | tf_op jit(solution)/shard_map/latent_attention/pallas_call | solution.py:358
  106.3 1.0 convert.8
  107.3 0.8 convert_element_type.10
  (4 shorter events, 0.1 us)
Async XLA Ops:
  0.0 3.4 %copy-start = (bf16[128,4,576]{0,2,1:T(8,128)(2,1)S(1)}, bf16[128,4,576]{0,2,1:T(8,128)(2,1)}, u32[]{:S(2)}) copy-start(bf16[128,4,576]{0,2,1:T(8,128)(2,1)} %param.4) | copy-start | bytes 1769476

commit v2 on v1

v2 whole, which is shorter than its diff:
```python
import functools

import jax
import jax.numpy as jnp
from jax import lax
from jax.experimental import pallas as pl
from jax.experimental.pallas import tpu as pltpu
from jax.sharding import PartitionSpec as P

MESH = pl.DeviceIdType.MESH
PIECE = 32
RELAYS = 3
LOG2E = 1.4426950408889634
score_scale = 192.0 ** (-0.5)
LOW = -1e30


def kernel(
    nz, nx, nvl,
    q_ref, lat_ref, up_ref, w_ref, out_ref,
    q_s, lat_s, wab, m_s, l_s, acc, vx, ps, cr, xs, xr, ys, yr,
    zl_s, zl_r, xl_s, xl_r, yf_s, yf_r, ce_s, ce_r, co_s, co_r,
    zw_s, zw_r, v_s, v_r, c_s, c_r, x_s, x_r, y_s, y_r,
):
    half = nz // 2
    lat, tok = lat_ref.shape
    hrow, prow = lat // 2, lat // 4
    heads, _, vd = up_ref.shape
    ncol = w_ref.shape[0]
    pieces = ncol // PIECE

    ctx, ex = lax.axis_index("ctx"), lax.axis_index("exp")
    z, yl = ctx // 2, ctx % 2
    yh, x, k = ex // (2 * nx), (ex // 2) % nx, ex % 2
    y = yh * 2 + yl

    def dev(zz=z, yy=y, xx=x, kk=k):
        return {"ctx": zz * 2 + yy % 2, "exp": (yy // 2) * (2 * nx) + xx * 2 + kk}

    zn = (dev(zz=(z + 1) % nz), dev(zz=(z + nz - 1) % nz))
    yn = (dev(yy=(y + 1) % 4), dev(yy=(y + 3) % 4))
    xl_to = (dev(xx=(x + 1) % nx), dev(xx=(x + nx - 1) % nx))
    core = dev(kk=1 - k)
    ypair = dev(yy=yh * 2 + 1 - yl)
    xn = tuple(((x + dx) % nx, dev(xx=(x + dx) % nx)) for dx in range(1, nx))
    y4 = tuple(((y + dy) % 4, dev(yy=(y + dy) % 4)) for dy in range(1, 4))

    def rc(src, dst, ss, rs, to):
        return pltpu.make_async_remote_copy(
            src_ref=src, dst_ref=dst, send_sem=ss, recv_sem=rs, device_id=to, device_id_type=MESH
        )

    def zc(d, s):
        return (z + nz - s) % nz if d == 0 else (z + s) % nz

    def reaches(s, d):
        return (s < half) | ((s == half) & (k == d))

    def lanes(yy):
        return pl.ds(pl.multiple_of(yy * tok, tok), tok)

    half_rows = pl.ds(pl.multiple_of(k * hrow, hrow), hrow)
    other_rows = pl.ds(pl.multiple_of((1 - k) * hrow, hrow), hrow)
    part_rows = pl.ds(pl.multiple_of(k * hrow + (x % 2) * prow, prow), prow)
    missing_rows = pl.ds(pl.multiple_of(k * hrow + (1 - x % 2) * prow, prow), prow)

    def zl(d, s, src=None, back=0):
        at = lat_s.at[zc(d, s), part_rows, lanes(yl)]
        return rc(at if src is None else src, at, zl_s.at[d, s - back], zl_r.at[d, s - back], zn[d])

    def xl(d, s, rows):
        at = lat_s.at[zc(d, s), rows, lanes(yl)]
        return rc(at, at, xl_s.at[d, s], xl_r.at[d, s], xl_to[d])

    def yf(d, s, yy, src=None):
        at = lat_s.at[zc(d, s), half_rows, lanes(yy)]
        return rc(at if src is None else src, at, yf_s.at[d, s], yf_r.at[d, s], yn[d])

    def ce(d, s, rows):
        at = lat_s.at[zc(d, s), rows, lanes(yl)]
        return rc(at, at, ce_s.at[d, s], ce_r.at[d, s], core)

    def co(d, s, rows):
        at = lat_s.at[zc(d, s), rows, lanes(1 - yl)]
        return rc(at, at, co_s.at[d, s], co_r.at[d, s], core)

    def zw(d, n, back=0, own=False):
        rows = pl.ds(pl.multiple_of((n % pieces) * PIECE, PIECE), PIECE)
        at = wab.at[zc(d, n // pieces), rows]
        m = n - back
        return rc(w_ref.at[rows] if own else at, at, zw_s.at[d, m], zw_r.at[d, m], zn[d])

    def relay(n):
        s = n // pieces
        for d in range(2):
            @pl.when((s >= 1) & reaches(s, d))
            def _():
                zw(d, n, back=pieces).wait_recv()

        for d in range(2):
            @pl.when((n >= 2) & reaches((n - 2) // pieces + 1, d))
            def _():
                zw(d, n - 2).wait_send()

            @pl.when((s >= 1) & reaches(s + 1, d))
            def _():
                zw(d, n).start()

            @pl.when(s == 0)
            def _():
                zw(d, n, own=True).start()

    barrier = pltpu.get_barrier_semaphore()
    peers = [zn[0], zn[1], core] + [t for _, t in xn] + [t for _, t in y4]
    for peer in peers:
        pl.semaphore_signal(barrier, inc=1, device_id=peer, device_id_type=MESH)
    pl.semaphore_wait(barrier, len(peers))

    for d in range(2):
        zl(d, 0, lat_ref.at[part_rows]).start()
    yf(0, 0, yl, lat_ref.at[half_rows]).start()
    for n in range(RELAYS):
        relay(jnp.int32(n))

    for side in range(2):
        @pl.when(yl == side)
        def _():
            lat_s[z, :, side * tok:(side + 1) * tok] = lat_ref[...]
    wab[z] = w_ref[...]
    eye = (
        lax.broadcasted_iota(jnp.int32, (tok, tok), 0)
        == lax.broadcasted_iota(jnp.int32, (tok, tok), 1)
    ).astype(jnp.bfloat16)
    for h in range(heads):
        q_s[h * tok:(h + 1) * tok, :] = lax.dot_general(
            eye, q_ref[h], (((1,), (1,)), ((), ())), preferred_element_type=jnp.float32
        ).astype(jnp.bfloat16)
    m_s[...] = jnp.full_like(m_s, LOW)
    l_s[...] = jnp.zeros_like(l_s)
    acc[...] = jnp.zeros_like(acc)

    def attend(c):
        scores = jnp.dot(
            q_s[...], lat_s[c], preferred_element_type=jnp.float32
        ) * (score_scale * LOG2E)
        rows, cols = scores.shape
        row_pos = z * cols + yl * tok + lax.broadcasted_iota(jnp.int32, (rows, cols), 0) % tok
        key_pos = c * cols + lax.broadcasted_iota(jnp.int32, (rows, cols), 1)
        scores = jnp.where(key_pos <= row_pos, scores, LOW)
        old = m_s[...]
        new = jnp.maximum(old, jnp.max(scores, axis=1, keepdims=True))
        shrink = jnp.exp2(old - new)
        expo = jnp.exp2(scores - new)
        m_s[...] = new
        l_s[...] = l_s[...] * shrink + jnp.sum(expo, axis=1, keepdims=True)
        acc[...] = acc[...] * shrink + lax.dot_general(
            expo.astype(jnp.bfloat16), lat_s[c, :nvl], (((1,), (1,)), ((), ())),
            preferred_element_type=jnp.float32,
        )

    steps = half + 3

    @pl.loop(1, steps + 1)
    def _(s):
        for d in range(2):
            @pl.when(reaches(s, d))
            def _():
                zl(d, s, back=1).wait_recv()

                @pl.when(reaches(s + 1, d))
                def _():
                    zl(d, s).start()

                xl(d, s, part_rows).start()

        relay(RELAYS * s)

        s1 = s - 1
        for d in range(2):
            @pl.when((s1 >= 1) & reaches(s1, d))
            def _():
                xl(d, s1, missing_rows).wait_recv()
                yf(d, s1, yl).start()
                ce(d, s1, half_rows).start()

        s2 = s - 2
        for d in range(2):
            @pl.when(((s2 == 0) & (d == 0)) | ((s2 >= 1) & reaches(s2, d)))
            def _():
                yf(d, s2, 1 - yl).wait_recv()
                co(d, s2, half_rows).start()

        for r in range(1, RELAYS):
            relay(RELAYS * s + r)

        s3 = s - 3
        for d in range(2):
            there = (s3 >= 1) & reaches(s3, 1 - d)

            @pl.when(there)
            def _():
                ce(d, s3, other_rows).wait_recv()

            @pl.when(there | ((s3 == 0) & (d == 0)))
            def _():
                co(d, s3, other_rows).wait_recv()

        @pl.loop(0, 2)
        def _(d):
            c = jnp.where(d == 0, z - s3, z + s3 - nz)

            @pl.when((s3 >= 0) & (c >= 0) & ((d == 0) | ((s3 >= 1) & (s3 < half))))
            def _():
                attend(c)

    for h in range(heads):
        rows = pl.ds(h * tok, tok)
        context = (acc[rows, :] / l_s[rows, :]).astype(jnp.bfloat16)
        vx[yl, :, h * vd:(h + 1) * vd] = jnp.dot(
            context, up_ref[h], preferred_element_type=jnp.float32
        ).astype(jnp.bfloat16)

    rc(vx.at[yl], vx.at[yl], v_s, v_r, ypair).start()
    rc(vx.at[1 - yl], vx.at[1 - yl], v_s, v_r, ypair).wait_recv()

    def block_of(g, j):
        far = g == half - 1
        return zc(0, jnp.where(far, 0, g + 1)) if j == 0 else zc(1, jnp.where(far, half, g + 1))

    def c_copy(g):
        return rc(ps.at[g, 1 - k], cr.at[g], c_s.at[g], c_r.at[g], core)

    def x_copy(g, dx):
        at, to = xn[dx]
        return rc(xs.at[g, at], xr.at[g, dx], x_s.at[g, dx], x_r.at[g, dx], to)

    def y_copy(g, dy):
        at, to = y4[dy]
        return rc(ys.at[g, at], yr.at[g, dy], y_s.at[g, dy], y_r.at[g, dy], to)

    def part(g):
        both = vx[...].reshape(2 * tok, vx.shape[2])
        for j in range(2):
            o = lax.dot_general(
                both, wab[block_of(g, j)], (((1,), (1,)), ((), ())),
                preferred_element_type=jnp.float32,
            )
            o = o.reshape(2, tok // 16, 2, 8, ncol)
            for kk in range(2):
                piece = jnp.concatenate([o[0, :, kk], o[1, :, kk]], axis=1)
                ps[g, kk, :, j] = piece.astype(jnp.bfloat16)
        c_copy(g).start()

    def sum_cores(g):
        c_copy(g).wait_recv()
        s = ps[g, k].astype(jnp.float32) + cr[g].astype(jnp.float32)
        s = s.astype(jnp.bfloat16)
        for hi in range(2):
            xs[g, :, hi] = s[hi * nx:(hi + 1) * nx]
        for dx in range(nx - 1):
            x_copy(g, dx).start()

    def sum_x(g):
        t = xs[g, x].astype(jnp.float32)
        for dx in range(nx - 1):
            x_copy(g, dx).wait_recv()
            t = t + xr[g, dx].astype(jnp.float32)
        for hi in range(2):
            for lo in range(2):
                ys[g, hi * 2 + lo] = t[hi, :, lo * 8:(lo + 1) * 8]
        for dy in range(3):
            y_copy(g, dy).start()

    def sum_y(g):
        for dy in range(3):
            y_copy(g, dy).wait_recv()
        own = (ys[g, y] + yr[g, 1]).astype(out_ref.dtype)
        other = (yr[g, 0] + yr[g, 2]).astype(out_ref.dtype)
        for j in range(2):
            c = block_of(g, j)
            out_ref[2 * c + yl] = own[j]
            out_ref[2 * c + 1 - yl] = other[j]

    done = RELAYS * (steps + 1)
    last = half * pieces + pieces - 1
    first = max(0, min(half, done // pieces - 1))
    late = half - first
    begin = max((first + 1) * pieces + pieces - 1 - done, first)
    gap = max(first, 3)
    stages = (part, sum_cores, sum_x, sum_y)
    ticks = max(last - done + 1, 4 * first, begin + 3 * gap + (late - 1) * pieces + 1 if late else 0)

    @pl.loop(0, ticks)
    def _(t):
        @pl.when(t + done <= last)
        def _():
            relay(t + done)

        for i, stage in enumerate(stages):
            u = t - begin - i * gap
            early = (t >= i * first) & (t < (i + 1) * first)
            after = (u >= 0) & (u % pieces == 0) & (u < late * pieces)

            @pl.when(early | after)
            def _():
                stage(jnp.where(early, t - i * first, first + u // pieces))

    @pl.loop(0, half + 1)
    def _(s):
        for d in range(2):
            @pl.when(reaches(s + 1, d))
            def _():
                zl(d, s).wait_send()

            got = (s >= 1) & reaches(s, d)

            @pl.when(got)
            def _():
                xl(d, s, part_rows).wait_send()
                ce(d, s, half_rows).wait_send()

            @pl.when(got | ((s == 0) & (d == 0)))
            def _():
                yf(d, s, yl).wait_send()
                co(d, s, half_rows).wait_send()

    rc(vx.at[yl], vx.at[yl], v_s, v_r, ypair).wait_send()

    @pl.loop(0, half)
    def _(g):
        c_copy(g).wait_send()
        for dx in range(nx - 1):
            x_copy(g, dx).wait_send()
        for dy in range(3):
            y_copy(g, dy).wait_send()


def shards(queries, latents, value_up, out_weight):
    nz = lax.axis_size("ctx") // 2
    nx = lax.axis_size("exp") // 4
    tok, heads, lat = queries.shape
    nvl, vd = value_up.shape[1], value_up.shape[2]
    rows = tok * heads
    width = heads * vd
    ncol = out_weight.shape[1]
    half = nz // 2
    ng = half
    bf, f32 = jnp.bfloat16, jnp.float32
    dma = pltpu.SemaphoreType.DMA
    vmem = pl.BlockSpec(memory_space=pltpu.VMEM)
    out = pl.pallas_call(
        functools.partial(kernel, nz, nx, nvl),
        out_shape=jax.ShapeDtypeStruct((2 * nz, 8, ncol), bf),
        in_specs=[vmem] * 4,
        out_specs=vmem,
        scratch_shapes=[
            pltpu.VMEM((rows, lat), bf),
            pltpu.VMEM((nz, lat, 2 * tok), bf),
            pltpu.VMEM((nz, ncol, width), bf),
            pltpu.VMEM((rows, 1), f32),
            pltpu.VMEM((rows, 1), f32),
            pltpu.VMEM((rows, nvl), f32),
            pltpu.VMEM((2, tok, width), bf),
            pltpu.VMEM((ng, 2, 2 * nx, 2, 16, ncol), bf),
            pltpu.VMEM((ng, 2 * nx, 2, 16, ncol), bf),
            pltpu.VMEM((ng, nx, 2, 2, 16, ncol), bf),
            pltpu.VMEM((ng, nx - 1, 2, 2, 16, ncol), bf),
            pltpu.VMEM((ng, 4, 2, 8, ncol), f32),
            pltpu.VMEM((ng, 3, 2, 8, ncol), f32),
        ]
        + [dma((2, half + 1))] * 10
        + [dma((2, half * (ncol // PIECE)))] * 2
        + [dma(())] * 2
        + [dma((ng,))] * 2
        + [dma((ng, nx - 1))] * 2
        + [dma((ng, 3))] * 2,
        compiler_params=pltpu.CompilerParams(
            collective_id=0, has_side_effects=True, vmem_limit_bytes=56 * 2**20
        ),
        name="latent_attention",
    )(jnp.transpose(queries, (1, 2, 0)), latents.T, value_up, out_weight.T)
    return jnp.moveaxis(out, 1, 0).reshape(8, 2 * nz * ncol)


def solution(mesh):
    in_specs = (P("ctx", "exp", None), P("ctx", None), P("exp", None, None), P("exp", "ctx"))
    out_specs = P(("ctx", "exp"), None)
    return jax.shard_map(shards, mesh=mesh, in_specs=in_specs, out_specs=out_specs, check_vma=False)
```

time: 108 us -> 101 us (0.935)
  local copies, waits for them, and re-layouts: 5.41 us -> 1.77 us
  Pallas kernels: 102 us -> 98.8 us
    pallas_call x1, Pallas kernels: 102 us -> 98.8 us  [shards(): pl.pallas_call(functools.partial(kernel, nz, nx, nvl), out_shape=jax.Shap...]
    unnamed x3 -> x0, local copies, waits for them, and re-layouts: 1.77 us -> none
    pad x1 -> x0, local copies, waits for them, and re-layouts: 1.66 us -> none  [shards(): jnp.pad(out_weight.T, ((0, 2 * LANES - ncol), (0, 0)))]
where the time goes in v2:
time: 101 us
  Pallas kernels  98.8 us (98%)
  local copies, waits for them, and re-layouts  1.77 us (2%)
    pallas_call x1, Pallas kernels, shards(): pl.pallas_call(functools.partial(kernel, nz, nx, nvl), out_shape=jax.Shap...  98.8 us

profile of v2, /device:TPU:1, one launch (start us, length us, event | category | flops | bytes accessed | tf_op | source)
XLA Modules:
  0.0 100.6 jit_solution(15746786888066580943)
XLA Ops:
  0.0 98.8 %latent_attention.1 = bf16[32,8,224]{2,1,0:T(8,128)(2,1)} custom-call(bf16[4,576,128]{2,1,0:T(8,128)(2,1)} %bitcast.4, bf16[576,128]{1,0:T(8,128)(2,1)} %bitcast.7, bf16[4,512,128]{2,1,0:T(8,128)(2,1)} %up_ref.1, bf16[224,512]{1,0:T(8,128)(2,1)} %bitcast.6), custom_call_target="tpu_custom_call" | custom-call | tf_op jit(solution)/shard_map/latent_attention/pallas_call | solution.py:351
  98.8 0.9 copy.5
  99.7 0.8 reshape.3

commit v3 on v2

--- a/solution.py
+++ b/solution.py
@@ -10,6 +10,7 @@
 MESH = pl.DeviceIdType.MESH
 PIECE = 32
 RELAYS = 3
+FLIGHT = 4
 LOG2E = 1.4426950408889634
 score_scale = 192.0 ** (-0.5)
 LOW = -1e30
@@ -18,15 +19,15 @@
 def kernel(
     nz, nx, nvl,
     q_ref, lat_ref, up_ref, w_ref, out_ref,
-    q_s, lat_s, wab, m_s, l_s, acc, vx, ps, cr, xs, xr, ys, yr,
+    q_s, lat_s, wab, m_s, l_s, acc, vx, ps, xr, ts, fr,
     zl_s, zl_r, xl_s, xl_r, yf_s, yf_r, ce_s, ce_r, co_s, co_r,
-    zw_s, zw_r, v_s, v_r, c_s, c_r, x_s, x_r, y_s, y_r,
+    zw_s, zw_r, zf_s, zf_r, v_s, v_r, r_s, r_r, f_s, f_r,
 ):
     half = nz // 2
     lat, tok = lat_ref.shape
     hrow, prow = lat // 2, lat // 4
     heads, _, vd = up_ref.shape
-    ncol = w_ref.shape[0]
+    ncol, width = w_ref.shape
     pieces = ncol // PIECE
 
     ctx, ex = lax.axis_index("ctx"), lax.axis_index("exp")
@@ -42,8 +43,11 @@
     xl_to = (dev(xx=(x + 1) % nx), dev(xx=(x + nx - 1) % nx))
     core = dev(kk=1 - k)
     ypair = dev(yy=yh * 2 + 1 - yl)
-    xn = tuple(((x + dx) % nx, dev(xx=(x + dx) % nx)) for dx in range(1, nx))
-    y4 = tuple(((y + dy) % 4, dev(yy=(y + dy) % 4)) for dy in range(1, 4))
+    ypair_core = dev(yy=yh * 2 + 1 - yl, kk=1 - k)
+    plane = tuple(
+        ((y + dy) % 4, (x + dx) % nx, dev(yy=(y + dy) % 4, xx=(x + dx) % nx))
+        for dy in range(4) for dx in range(nx) if dy or dx
+    )
 
     def rc(src, dst, ss, rs, to):
         return pltpu.make_async_remote_copy(
@@ -84,9 +88,22 @@
         at = lat_s.at[zc(d, s), rows, lanes(1 - yl)]
         return rc(at, at, co_s.at[d, s], co_r.at[d, s], core)
 
+    def wlanes(kk):
+        return pl.ds(pl.multiple_of(kk * width, width), width)
+
+    def zf(c, n, own=False):
+        rows = pl.ds(pl.multiple_of((n % pieces) * PIECE, PIECE), PIECE)
+        at = wab.at[c, rows, wlanes(k)]
+        s = n // pieces
+        return rc(w_ref.at[rows] if own else at, at, zf_s.at[s], zf_r.at[s], core)
+
+    def zf_block(c, s, kk):
+        at = wab.at[c, :, wlanes(kk)]
+        return rc(at, at, zf_s.at[s], zf_r.at[s], core)
+
     def zw(d, n, back=0, own=False):
         rows = pl.ds(pl.multiple_of((n % pieces) * PIECE, PIECE), PIECE)
-        at = wab.at[zc(d, n // pieces), rows]
+        at = wab.at[zc(d, n // pieces), rows, wlanes(k)]
         m = n - back
         return rc(w_ref.at[rows] if own else at, at, zw_s.at[d, m], zw_r.at[d, m], zn[d])
 
@@ -97,10 +114,18 @@
             def _():
                 zw(d, n, back=pieces).wait_recv()
 
-        for d in range(2):
-            @pl.when((n >= 2) & reaches((n - 2) // pieces + 1, d))
-            def _():
-                zw(d, n - 2).wait_send()
+                @pl.when(((s < half) & (k != d)) | ((s == half) & (k == 0)))
+                def _():
+                    zf(zc(d, s), n).start()
+
+        @pl.when((s == 0) & (k == 1))
+        def _():
+            zf(z, n, own=True).start()
+
+        for d in range(2):
+            @pl.when((n >= FLIGHT) & reaches((n - FLIGHT) // pieces + 1, d))
+            def _():
+                zw(d, n - FLIGHT).wait_send()
 
             @pl.when((s >= 1) & reaches(s + 1, d))
             def _():
@@ -111,7 +136,7 @@
                 zw(d, n, own=True).start()
 
     barrier = pltpu.get_barrier_semaphore()
-    peers = [zn[0], zn[1], core] + [t for _, t in xn] + [t for _, t in y4]
+    peers = [zn[0], zn[1], core, ypair_core] + [t for _, _, t in plane]
     for peer in peers:
         pl.semaphore_signal(barrier, inc=1, device_id=peer, device_id_type=MESH)
     pl.semaphore_wait(barrier, len(peers))
@@ -126,7 +151,10 @@
         @pl.when(yl == side)
         def _():
             lat_s[z, :, side * tok:(side + 1) * tok] = lat_ref[...]
-    wab[z] = w_ref[...]
+    for side in range(2):
+        @pl.when(k == side)
+        def _():
+            wab[z, :, side * width:(side + 1) * width] = w_ref[...]
     eye = (
         lax.broadcasted_iota(jnp.int32, (tok, tok), 0)
         == lax.broadcasted_iota(jnp.int32, (tok, tok), 1)
@@ -190,7 +218,7 @@
                 yf(d, s2, 1 - yl).wait_recv()
                 co(d, s2, half_rows).start()
 
-        for r in range(1, RELAYS):
+        for r in range(1, RELAYS - 1):
             relay(RELAYS * s + r)
 
         s3 = s - 3
@@ -213,73 +241,81 @@
             def _():
                 attend(c)
 
+            @pl.when(d == 0)
+            def _():
+                relay(RELAYS * s + RELAYS - 1)
+
+    made = []
     for h in range(heads):
         rows = pl.ds(h * tok, tok)
         context = (acc[rows, :] / l_s[rows, :]).astype(jnp.bfloat16)
-        vx[yl, :, h * vd:(h + 1) * vd] = jnp.dot(
-            context, up_ref[h], preferred_element_type=jnp.float32
+        made.append(
+            jnp.dot(context, up_ref[h], preferred_element_type=jnp.float32).astype(jnp.bfloat16)
+        )
+    made = jnp.concatenate(made, axis=1)
+    for side in range(2):
+        @pl.when(k == side)
+        def _():
+            vx[yl, :, side * width:(side + 1) * width] = made
+
+    def v_copy(i, yy, kk):
+        at = vx.at[yy, :, wlanes(kk)]
+        return rc(at, at, v_s.at[i], v_r.at[i], (core, ypair, ypair_core)[i])
+
+    for i in range(3):
+        v_copy(i, yl, k).start()
+    v_copy(0, yl, 1 - k).wait_recv()
+    v_copy(1, 1 - yl, k).wait_recv()
+    v_copy(2, 1 - yl, 1 - k).wait_recv()
+
+    def steps_of(g, kk):
+        return g + kk
+
+    def block_of(g, kk):
+        return jnp.where(kk == 0, zc(0, g), zc(1, g + 1))
+
+    def f_copy(g):
+        return rc(ts.at[g, 1 - k], fr.at[g], f_s.at[g], f_r.at[g], core)
+
+    def r_all(g):
+        return rc(xr.at[g], xr.at[g], r_s.at[g], r_r.at[g], core)
+
+    def part(g):
+        c = block_of(g, k)
+        zf_block(c, steps_of(g, k), 1 - k).wait_recv()
+        o = lax.dot_general(
+            vx[...].reshape(2 * tok, 2 * width), wab[c], (((1,), (1,)), ((), ())),
+            preferred_element_type=jnp.float32,
         ).astype(jnp.bfloat16)
-
-    rc(vx.at[yl], vx.at[yl], v_s, v_r, ypair).start()
-    rc(vx.at[1 - yl], vx.at[1 - yl], v_s, v_r, ypair).wait_recv()
-
-    def block_of(g, j):
-        far = g == half - 1
-        return zc(0, jnp.where(far, 0, g + 1)) if j == 0 else zc(1, jnp.where(far, half, g + 1))
-
-    def c_copy(g):
-        return rc(ps.at[g, 1 - k], cr.at[g], c_s.at[g], c_r.at[g], core)
-
-    def x_copy(g, dx):
-        at, to = xn[dx]
-        return rc(xs.at[g, at], xr.at[g, dx], x_s.at[g, dx], x_r.at[g, dx], to)
-
-    def y_copy(g, dy):
-        at, to = y4[dy]
-        return rc(ys.at[g, at], yr.at[g, dy], y_s.at[g, dy], y_r.at[g, dy], to)
-
-    def part(g):
-        both = vx[...].reshape(2 * tok, vx.shape[2])
-        for j in range(2):
-            o = lax.dot_general(
-                both, wab[block_of(g, j)], (((1,), (1,)), ((), ())),
-                preferred_element_type=jnp.float32,
-            )
-            o = o.reshape(2, tok // 16, 2, 8, ncol)
-            for kk in range(2):
-                piece = jnp.concatenate([o[0, :, kk], o[1, :, kk]], axis=1)
-                ps[g, kk, :, j] = piece.astype(jnp.bfloat16)
-        c_copy(g).start()
-
-    def sum_cores(g):
-        c_copy(g).wait_recv()
-        s = ps[g, k].astype(jnp.float32) + cr[g].astype(jnp.float32)
-        s = s.astype(jnp.bfloat16)
-        for hi in range(2):
-            xs[g, :, hi] = s[hi * nx:(hi + 1) * nx]
-        for dx in range(nx - 1):
-            x_copy(g, dx).start()
-
-    def sum_x(g):
-        t = xs[g, x].astype(jnp.float32)
-        for dx in range(nx - 1):
-            x_copy(g, dx).wait_recv()
-            t = t + xr[g, dx].astype(jnp.float32)
+        o = o.reshape(2, 2, nx, 16, ncol)
         for hi in range(2):
             for lo in range(2):
-                ys[g, hi * 2 + lo] = t[hi, :, lo * 8:(lo + 1) * 8]
-        for dy in range(3):
-            y_copy(g, dy).start()
-
-    def sum_y(g):
-        for dy in range(3):
-            y_copy(g, dy).wait_recv()
-        own = (ys[g, y] + yr[g, 1]).astype(out_ref.dtype)
-        other = (yr[g, 0] + yr[g, 2]).astype(out_ref.dtype)
-        for j in range(2):
-            c = block_of(g, j)
-            out_ref[2 * c + yl] = own[j]
-            out_ref[2 * c + 1 - yl] = other[j]
+                ps[g, hi * 2 + lo] = o[lo, hi]
+        for i, (yy, xx, to) in enumerate(plane):
+            rc(ps.at[g, yy, xx], xr.at[g, i], r_s.at[g], r_r.at[g], to).start()
+
+    def sum_plane(g):
+        r_all(g).wait_recv()
+        own, other = ps[g, y, x].astype(jnp.float32), None
+        for i in range(4 * nx - 1):
+            term = xr[g, i].astype(jnp.float32)
+            if ((i + 1) // nx) % 2 == 0:
+                own = own + term
+            else:
+                other = term if other is None else other + term
+        for side, total in enumerate((own, other)):
+            for kk in range(2):
+                ts[g, kk, side] = total[kk * 8:(kk + 1) * 8].astype(ts.dtype)
+        f_copy(g).start()
+        c = block_of(g, k)
+        out_ref[2 * c + yl] = ts[g, k, 0]
+        out_ref[2 * c + 1 - yl] = ts[g, k, 1]
+
+    def finish(g):
+        f_copy(g).wait_recv()
+        c = block_of(g, 1 - k)
+        out_ref[2 * c + yl] = fr[g, 0]
+        out_ref[2 * c + 1 - yl] = fr[g, 1]
 
     done = RELAYS * (steps + 1)
     last = half * pieces + pieces - 1
@@ -287,8 +323,8 @@
     late = half - first
     begin = max((first + 1) * pieces + pieces - 1 - done, first)
     gap = max(first, 3)
-    stages = (part, sum_cores, sum_x, sum_y)
-    ticks = max(last - done + 1, 4 * first, begin + 3 * gap + (late - 1) * pieces + 1 if late else 0)
+    stages = (part, sum_plane, finish)
+    ticks = max(last - done + 1, 3 * first, begin + 2 * gap + (late - 1) * pieces + 1 if late else 0)
 
     @pl.loop(0, ticks)
     def _(t):
@@ -324,15 +360,14 @@
                 yf(d, s, yl).wait_send()
                 co(d, s, half_rows).wait_send()
 
-    rc(vx.at[yl], vx.at[yl], v_s, v_r, ypair).wait_send()
+    for i in range(3):
+        v_copy(i, yl, k).wait_send()
 
     @pl.loop(0, half)
     def _(g):
-        c_copy(g).wait_send()
-        for dx in range(nx - 1):
-            x_copy(g, dx).wait_send()
-        for dy in range(3):
-            y_copy(g, dy).wait_send()
+        zf_block(block_of(g, 1 - k), steps_of(g, 1 - k), k).wait_send()
+        r_all(g).wait_send()
+        f_copy(g).wait_send()
 
 
 def shards(queries, latents, value_up, out_weight):
@@ -356,24 +391,21 @@
         scratch_shapes=[
             pltpu.VMEM((rows, lat), bf),
             pltpu.VMEM((nz, lat, 2 * tok), bf),
-            pltpu.VMEM((nz, ncol, width), bf),
+            pltpu.VMEM((nz, ncol, 2 * width), bf),
             pltpu.VMEM((rows, 1), f32),
             pltpu.VMEM((rows, 1), f32),
             pltpu.VMEM((rows, nvl), f32),
-            pltpu.VMEM((2, tok, width), bf),
-            pltpu.VMEM((ng, 2, 2 * nx, 2, 16, ncol), bf),
-            pltpu.VMEM((ng, 2 * nx, 2, 16, ncol), bf),
-            pltpu.VMEM((ng, nx, 2, 2, 16, ncol), bf),
-            pltpu.VMEM((ng, nx - 1, 2, 2, 16, ncol), bf),
-            pltpu.VMEM((ng, 4, 2, 8, ncol), f32),
-            pltpu.VMEM((ng, 3, 2, 8, ncol), f32),
+            pltpu.VMEM((2, tok, 2 * width), bf),
+            pltpu.VMEM((ng, 4, nx, 16, ncol), bf),
+            pltpu.VMEM((ng, 4 * nx - 1, 16, ncol), bf),
+            pltpu.VMEM((ng, 2, 2, 8, ncol), bf),
+            pltpu.VMEM((ng, 2, 8, ncol), bf),
         ]
         + [dma((2, half + 1))] * 10
         + [dma((2, half * (ncol // PIECE)))] * 2
-        + [dma(())] * 2
-        + [dma((ng,))] * 2
-        + [dma((ng, nx - 1))] * 2
-        + [dma((ng, 3))] * 2,
+        + [dma((half + 1,))] * 2
+        + [dma((3,))] * 2
+        + [dma((ng,))] * 4,
         compiler_params=pltpu.CompilerParams(
             collective_id=0, has_side_effects=True, vmem_limit_bytes=56 * 2**20
         ),

time: 101 us -> 98 us (0.970)
  Pallas kernels: 98.8 us -> 96.1 us
    pallas_call x1, Pallas kernels: 98.8 us -> 96.1 us  [shards(): pl.pallas_call(functools.partial(kernel, nz, nx, nvl), out_shape=jax.Shap...]
where the time goes in v3:
time: 98 us; the launch traced here: 97.8 us
  Pallas kernels  96.1 us (98%)
  local copies, waits for them, and re-layouts  1.77 us (2%)
    pallas_call x1, Pallas kernels, shards(): pl.pallas_call(functools.partial(kernel, nz, nx, nvl), out_shape=jax.Shap...  96.1 us

profile of v3, /device:TPU:1, one launch (start us, length us, event | category | flops | bytes accessed | tf_op | source)
XLA Modules:
  0.0 97.8 jit_solution(16114255518590049807)
XLA Ops:
  0.0 96.1 %latent_attention.1 = bf16[32,8,224]{2,1,0:T(8,128)(2,1)} custom-call(bf16[4,576,128]{2,1,0:T(8,128)(2,1)} %bitcast.4, bf16[576,128]{1,0:T(8,128)(2,1)} %bitcast.7, bf16[4,512,128]{2,1,0:T(8,128)(2,1)} %up_ref.1, bf16[224,512]{1,0:T(8,128)(2,1)} %bitcast.6), custom_call_target="tpu_custom_call" | custom-call | tf_op jit(solution)/shard_map/latent_attention/pallas_call | solution.py:386
  96.1 0.9 copy.5
  97.0 0.8 reshape.3

commit v4 on v3

--- a/solution.py
+++ b/solution.py
@@ -8,12 +8,47 @@
 from jax.sharding import PartitionSpec as P
 
 MESH = pl.DeviceIdType.MESH
-PIECE = 32
-RELAYS = 3
-FLIGHT = 4
+PIECE = 112
+FLIGHT = 2
 LOG2E = 1.4426950408889634
 score_scale = 192.0 ** (-0.5)
 LOW = -1e30
+
+
+def when(*conditions):
+    if any(c is False for c in conditions):
+        return lambda body: None
+    traced = [c for c in conditions if c is not True]
+    if not traced:
+        return lambda body: body()
+    return pl.when(functools.reduce(lambda a, b: a & b, traced))
+
+
+def order_of(relays, groups, ready_after):
+    pace, exchange, swap = 2.75, 5.5, 1.6
+    costs = {"part": 1.0, "sum": 0.5, "end": 0.2, "relay": 0.1}
+    now, out, n, p = 0.0, [], 0, 0
+    sums, ends = [], []
+    while len([o for o in out if o[0] == "end"]) < groups or n < len(relays):
+        if n < len(relays) and now >= (n + 1) * pace:
+            step = ("relay", relays[n])
+            n += 1
+        elif p < groups and ready_after[p] <= n:
+            step = ("part", p)
+            sums.append((now + exchange, p))
+            p += 1
+        elif sums and now >= sums[0][0]:
+            step = ("sum", sums[0][1])
+            ends.append((now + swap, sums.pop(0)[1]))
+        elif ends and now >= ends[0][0]:
+            step = ("end", ends.pop(0)[1])
+        else:
+            waits = [(n + 1) * pace] * (n < len(relays)) + [q[0] for q in sums[:1] + ends[:1]]
+            now = max(now, min(waits)) + 1e-6
+            continue
+        now += costs[step[0]]
+        out.append(step)
+    return out
 
 
 def kernel(
@@ -58,7 +93,7 @@
         return (z + nz - s) % nz if d == 0 else (z + s) % nz
 
     def reaches(s, d):
-        return (s < half) | ((s == half) & (k == d))
+        return True if s < half else (k == d if s == half else False)
 
     def lanes(yy):
         return pl.ds(pl.multiple_of(yy * tok, tok), tok)
@@ -92,7 +127,7 @@
         return pl.ds(pl.multiple_of(kk * width, width), width)
 
     def zf(c, n, own=False):
-        rows = pl.ds(pl.multiple_of((n % pieces) * PIECE, PIECE), PIECE)
+        rows = pl.ds((n % pieces) * PIECE, PIECE)
         at = wab.at[c, rows, wlanes(k)]
         s = n // pieces
         return rc(w_ref.at[rows] if own else at, at, zf_s.at[s], zf_r.at[s], core)
@@ -102,7 +137,7 @@
         return rc(at, at, zf_s.at[s], zf_r.at[s], core)
 
     def zw(d, n, back=0, own=False):
-        rows = pl.ds(pl.multiple_of((n % pieces) * PIECE, PIECE), PIECE)
+        rows = pl.ds((n % pieces) * PIECE, PIECE)
         at = wab.at[zc(d, n // pieces), rows, wlanes(k)]
         m = n - back
         return rc(w_ref.at[rows] if own else at, at, zw_s.at[d, m], zw_r.at[d, m], zn[d])
@@ -110,30 +145,26 @@
     def relay(n):
         s = n // pieces
         for d in range(2):
-            @pl.when((s >= 1) & reaches(s, d))
+            @when(s >= 1, reaches(s, d))
             def _():
                 zw(d, n, back=pieces).wait_recv()
 
-                @pl.when(((s < half) & (k != d)) | ((s == half) & (k == 0)))
+                @pl.when(k != d if s < half else k == 0)
                 def _():
                     zf(zc(d, s), n).start()
 
-        @pl.when((s == 0) & (k == 1))
+        @when(s == 0, k == 1)
         def _():
             zf(z, n, own=True).start()
 
         for d in range(2):
-            @pl.when((n >= FLIGHT) & reaches((n - FLIGHT) // pieces + 1, d))
+            @when(n >= FLIGHT, reaches((n - FLIGHT) // pieces + 1, d))
             def _():
                 zw(d, n - FLIGHT).wait_send()
 
-            @pl.when((s >= 1) & reaches(s + 1, d))
-            def _():
-                zw(d, n).start()
-
-            @pl.when(s == 0)
-            def _():
-                zw(d, n, own=True).start()
+            @when(reaches(s + 1, d))
+            def _():
+                zw(d, n, own=s == 0).start()
 
     barrier = pltpu.get_barrier_semaphore()
     peers = [zn[0], zn[1], core, ypair_core] + [t for _, _, t in plane]
@@ -144,8 +175,7 @@
     for d in range(2):
         zl(d, 0, lat_ref.at[part_rows]).start()
     yf(0, 0, yl, lat_ref.at[half_rows]).start()
-    for n in range(RELAYS):
-        relay(jnp.int32(n))
+    relay(0)
 
     for side in range(2):
         @pl.when(yl == side)
@@ -167,14 +197,14 @@
     l_s[...] = jnp.zeros_like(l_s)
     acc[...] = jnp.zeros_like(acc)
 
-    def attend(c):
+    def attend(c, diagonal):
         scores = jnp.dot(
             q_s[...], lat_s[c], preferred_element_type=jnp.float32
         ) * (score_scale * LOG2E)
-        rows, cols = scores.shape
-        row_pos = z * cols + yl * tok + lax.broadcasted_iota(jnp.int32, (rows, cols), 0) % tok
-        key_pos = c * cols + lax.broadcasted_iota(jnp.int32, (rows, cols), 1)
-        scores = jnp.where(key_pos <= row_pos, scores, LOW)
+        if diagonal:
+            row_pos = yl * tok + lax.broadcasted_iota(jnp.int32, scores.shape, 0) % tok
+            key_pos = lax.broadcasted_iota(jnp.int32, scores.shape, 1)
+            scores = jnp.where(key_pos <= row_pos, scores, LOW)
         old = m_s[...]
         new = jnp.maximum(old, jnp.max(scores, axis=1, keepdims=True))
         shrink = jnp.exp2(old - new)
@@ -188,24 +218,21 @@
 
     steps = half + 3
 
-    @pl.loop(1, steps + 1)
-    def _(s):
-        for d in range(2):
-            @pl.when(reaches(s, d))
+    for s in range(1, steps + 1):
+        for d in range(2):
+            @when(reaches(s, d))
             def _():
                 zl(d, s, back=1).wait_recv()
 
-                @pl.when(reaches(s + 1, d))
+                @when(reaches(s + 1, d))
                 def _():
                     zl(d, s).start()
 
                 xl(d, s, part_rows).start()
 
-        relay(RELAYS * s)
-
         s1 = s - 1
         for d in range(2):
-            @pl.when((s1 >= 1) & reaches(s1, d))
+            @when(s1 >= 1, reaches(s1, d))
             def _():
                 xl(d, s1, missing_rows).wait_recv()
                 yf(d, s1, yl).start()
@@ -213,37 +240,35 @@
 
         s2 = s - 2
         for d in range(2):
-            @pl.when(((s2 == 0) & (d == 0)) | ((s2 >= 1) & reaches(s2, d)))
+            @when(s2 >= 1 or (s2 == 0 and d == 0), s2 == 0 or reaches(s2, d))
             def _():
                 yf(d, s2, 1 - yl).wait_recv()
                 co(d, s2, half_rows).start()
 
-        for r in range(1, RELAYS - 1):
-            relay(RELAYS * s + r)
+        relay(s)
 
         s3 = s - 3
         for d in range(2):
-            there = (s3 >= 1) & reaches(s3, 1 - d)
-
-            @pl.when(there)
+            there = reaches(s3, 1 - d)
+
+            @when(s3 >= 1, there)
             def _():
                 ce(d, s3, other_rows).wait_recv()
 
-            @pl.when(there | ((s3 == 0) & (d == 0)))
+            @when(s3 >= 1 or (s3 == 0 and d == 0), s3 == 0 or there)
             def _():
                 co(d, s3, other_rows).wait_recv()
 
-        @pl.loop(0, 2)
-        def _(d):
-            c = jnp.where(d == 0, z - s3, z + s3 - nz)
-
-            @pl.when((s3 >= 0) & (c >= 0) & ((d == 0) | ((s3 >= 1) & (s3 < half))))
-            def _():
-                attend(c)
-
-            @pl.when(d == 0)
-            def _():
-                relay(RELAYS * s + RELAYS - 1)
+        if s3 == 0:
+            attend(z, True)
+        if s3 >= 1:
+            @pl.loop(0, 2 if s3 < half else 1)
+            def _(d):
+                c = jnp.where(d == 0, z - s3, z + s3 - nz)
+
+                @pl.when(c >= 0)
+                def _():
+                    attend(c, False)
 
     made = []
     for h in range(heads):
@@ -317,45 +342,24 @@
         out_ref[2 * c + yl] = fr[g, 0]
         out_ref[2 * c + 1 - yl] = fr[g, 1]
 
-    done = RELAYS * (steps + 1)
-    last = half * pieces + pieces - 1
-    first = max(0, min(half, done // pieces - 1))
-    late = half - first
-    begin = max((first + 1) * pieces + pieces - 1 - done, first)
-    gap = max(first, 3)
-    stages = (part, sum_plane, finish)
-    ticks = max(last - done + 1, 3 * first, begin + 2 * gap + (late - 1) * pieces + 1 if late else 0)
-
-    @pl.loop(0, ticks)
-    def _(t):
-        @pl.when(t + done <= last)
-        def _():
-            relay(t + done)
-
-        for i, stage in enumerate(stages):
-            u = t - begin - i * gap
-            early = (t >= i * first) & (t < (i + 1) * first)
-            after = (u >= 0) & (u % pieces == 0) & (u < late * pieces)
-
-            @pl.when(early | after)
-            def _():
-                stage(jnp.where(early, t - i * first, first + u // pieces))
-
-    @pl.loop(0, half + 1)
-    def _(s):
-        for d in range(2):
-            @pl.when(reaches(s + 1, d))
+    relays = list(range(steps + 1, half * pieces + pieces))
+    ready_after = [max(0, (g + 2) * pieces - (steps + 1)) for g in range(half)]
+    stages = {"part": part, "sum": sum_plane, "end": finish, "relay": relay}
+    for name, index in order_of(relays, half, ready_after):
+        stages[name](index)
+
+    for s in range(half + 1):
+        for d in range(2):
+            @when(reaches(s + 1, d))
             def _():
                 zl(d, s).wait_send()
 
-            got = (s >= 1) & reaches(s, d)
-
-            @pl.when(got)
+            @when(s >= 1, reaches(s, d))
             def _():
                 xl(d, s, part_rows).wait_send()
                 ce(d, s, half_rows).wait_send()
 
-            @pl.when(got | ((s == 0) & (d == 0)))
+            @when(s >= 1 or d == 0, s == 0 or reaches(s, d))
             def _():
                 yf(d, s, yl).wait_send()
                 co(d, s, half_rows).wait_send()
@@ -363,8 +367,7 @@
     for i in range(3):
         v_copy(i, yl, k).wait_send()
 
-    @pl.loop(0, half)
-    def _(g):
+    for g in range(half):
         zf_block(block_of(g, 1 - k), steps_of(g, 1 - k), k).wait_send()
         r_all(g).wait_send()
         f_copy(g).wait_send()

time: 98 us -> 88.8 us (0.906)
  Pallas kernels: 96.1 us -> 86.9 us
    pallas_call x1, Pallas kernels: 96.1 us -> 86.9 us  [shards(): pl.pallas_call(functools.partial(kernel, nz, nx, nvl), out_shape=jax.Shap...]
where the time goes in v4:
time: 88.8 us; the launch traced here: 88.6 us
  Pallas kernels  86.9 us (98%)
  local copies, waits for them, and re-layouts  1.77 us (2%)
    pallas_call x1, Pallas kernels, shards(): pl.pallas_call(functools.partial(kernel, nz, nx, nvl), out_shape=jax.Shap...  86.9 us

profile of v4, /device:TPU:1, one launch (start us, length us, event | category | flops | bytes accessed | tf_op | source)
XLA Modules:
  0.0 88.6 jit_solution(7461459229938319254)
XLA Ops:
  0.0 86.9 %latent_attention.1 = bf16[32,8,224]{2,1,0:T(8,128)(2,1)} custom-call(bf16[4,576,128]{2,1,0:T(8,128)(2,1)} %bitcast.4, bf16[576,128]{1,0:T(8,128)(2,1)} %bitcast.7, bf16[4,512,128]{2,1,0:T(8,128)(2,1)} %up_ref.1, bf16[224,512]{1,0:T(8,128)(2,1)} %bitcast.6), custom_call_target="tpu_custom_call" | custom-call | tf_op jit(solution)/shard_map/latent_attention/pallas_call | solution.py:389
  86.9 0.9 %copy.5 = bf16[8,32,224]{2,1,0:T(8,128)(2,1)S(1)} copy(bf16[8,32,224]{2,0,1:T(8,128)(2,1)} %bitcast.5) | data formatting | bytes 229376 | tf_op jit(solution)/shard_map/transpose | solution.py:417
  87.8 0.8 reshape.3

commit v5 on v4

--- a/solution.py
+++ b/solution.py
@@ -9,6 +9,7 @@
 
 MESH = pl.DeviceIdType.MESH
 PIECE = 112
+EXTRA = (3, 6, 9)
 FLIGHT = 2
 LOG2E = 1.4426950408889634
 score_scale = 192.0 ** (-0.5)
@@ -218,6 +219,7 @@
 
     steps = half + 3
 
+    begun = 1
     for s in range(1, steps + 1):
         for d in range(2):
             @when(reaches(s, d))
@@ -245,7 +247,8 @@
                 yf(d, s2, 1 - yl).wait_recv()
                 co(d, s2, half_rows).start()
 
-        relay(s)
+        relay(begun)
+        begun += 1
 
         s3 = s - 3
         for d in range(2):
@@ -269,6 +272,10 @@
                 @pl.when(c >= 0)
                 def _():
                     attend(c, False)
+
+        if s in EXTRA and begun < half * pieces:
+            relay(begun)
+            begun += 1
 
     made = []
     for h in range(heads):
@@ -316,7 +323,8 @@
         for hi in range(2):
             for lo in range(2):
                 ps[g, hi * 2 + lo] = o[lo, hi]
-        for i, (yy, xx, to) in enumerate(plane):
+        for i in sorted(range(len(plane)), key=lambda i: -((i + 1) // nx == 2) - ((i + 1) % nx == 2)):
+            yy, xx, to = plane[i]
             rc(ps.at[g, yy, xx], xr.at[g, i], r_s.at[g], r_r.at[g], to).start()
 
     def sum_plane(g):
@@ -342,8 +350,8 @@
         out_ref[2 * c + yl] = fr[g, 0]
         out_ref[2 * c + 1 - yl] = fr[g, 1]
 
-    relays = list(range(steps + 1, half * pieces + pieces))
-    ready_after = [max(0, (g + 2) * pieces - (steps + 1)) for g in range(half)]
+    relays = list(range(begun, half * pieces + pieces))
+    ready_after = [max(0, (g + 2) * pieces - begun) for g in range(half)]
     stages = {"part": part, "sum": sum_plane, "end": finish, "relay": relay}
     for name, index in order_of(relays, half, ready_after):
         stages[name](index)

time: 88.8 us -> 86.1 us (0.970)
  Pallas kernels: 86.9 us -> 84.2 us
    pallas_call x1, Pallas kernels: 86.9 us -> 84.2 us  [shards(): pl.pallas_call(functools.partial(kernel, nz, nx, nvl), out_shape=jax.Shap...]
where the time goes in v5:
time: 86.1 us; the launch traced here: 86 us
  Pallas kernels  84.2 us (98%)
  local copies, waits for them, and re-layouts  1.77 us (2%)
    pallas_call x1, Pallas kernels, shards(): pl.pallas_call(functools.partial(kernel, nz, nx, nvl), out_shape=jax.Shap...  84.2 us

profile of v5, /device:TPU:1, one launch (start us, length us, event | category | flops | bytes accessed | tf_op | source)
XLA Modules:
  0.0 86.0 jit_solution(18017022098386579495)
XLA Ops:
  0.0 84.2 %latent_attention.1 = bf16[32,8,224]{2,1,0:T(8,128)(2,1)} custom-call(bf16[4,576,128]{2,1,0:T(8,128)(2,1)} %bitcast.4, bf16[576,128]{1,0:T(8,128)(2,1)} %bitcast.7, bf16[4,512,128]{2,1,0:T(8,128)(2,1)} %up_ref.1, bf16[224,512]{1,0:T(8,128)(2,1)} %bitcast.6), custom_call_target="tpu_custom_call" | custom-call | tf_op jit(solution)/shard_map/latent_attention/pallas_call | solution.py:397
  84.2 0.9 %copy.5 = bf16[8,32,224]{2,1,0:T(8,128)(2,1)S(1)} copy(bf16[8,32,224]{2,0,1:T(8,128)(2,1)} %bitcast.5) | data formatting | bytes 229376 | tf_op jit(solution)/shard_map/transpose | solution.py:425
  85.1 0.8 reshape.3
